TPU v7x, 32 devices: a whole 2x2x4 slice. The times are simulated.
32 devices in a mesh: pb: 4 (over y, core), ma: 8 (over z, x).
Axes of the slice: x: 2, y: 2, z: 4, core: 2. Of those that a mesh axis runs over, the one named last changes fastest.
Arguments:
- queries: bfloat16 [1, 1024, 2048], P(None, ('pb', 'ma')), may hold values from -6 to 6
- map_descriptors: bfloat16 [8192, 2048], P('ma', 'pb'), may hold values from -0.125 to 0.125
- slopes: int32 [8], replicated, may hold values from 0 to 15, as said below
Outputs:
- best: float32 [1, 1024, 8192], P(None, 'pb', 'ma')
Inputs may be any that keep to these rules, and one draw needn't show every extreme that they name: `slopes`: 8 distinct velocities; the largest is exactly 15.
All inputs are finite; a program needn't handle non-finite values.
Results may differ from a plain program's by a relative error of at most 0.0003.
Values may be sent and summed in bfloat16 or wider, within the bound.
A program may use at most 64 MiB of HBM per device.

v0:
```python
import math
import jax
import jax.numpy as jnp
from jax import lax
from jax.sharding import PartitionSpec as P

SEQ = 20
RAD = 10
SPAN = 285


def padded(value, sides, width):
    for axis, dim in sides:
        peers, length = (lax.axis_size(axis), value.shape[dim])
        up = [(i, (i + 1) % peers) for i in range(peers - 1)]
        down = [(j, i) for i, j in up]
        last = lax.slice_in_dim(value, length - width, length, axis=dim)
        leading = lax.slice_in_dim(value, 0, width, axis=dim)
        before = lax.ppermute(last, axis, up)
        after = lax.ppermute(leading, axis, down)
        value = jnp.concatenate([before, value, after], axis=dim)
    return value


def passed_along(value, axis, by):
    peers = lax.axis_size(axis)
    pairs = [(i, i + by) for i in range(peers) if 0 <= i + by < peers]
    return lax.ppermute(value, axis, pairs)


def score_tile(queries, map_descriptors):
    query_full = lax.all_gather(queries, "ma", axis=1, tiled=True)
    return jnp.einsum(
        "sqd,md->sqm",
        query_full,
        lax.all_gather(map_descriptors, "pb", axis=1, tiled=True),
        preferred_element_type=jnp.float32,
    )


def contrast(extended, columns):
    shape_out = (extended.shape[0], extended.shape[1], columns)
    running = jnp.zeros(shape_out, jnp.float32)
    squares = jnp.zeros(shape_out, jnp.float32)
    for offset in range(2 * RAD + 1):
        window = extended[:, :, offset : offset + columns]
        running = running + window
        squares = squares + window * window
    average = running / (2 * RAD + 1)
    spread = squares / (2 * RAD + 1) - average * average
    centre = extended[:, :, RAD : RAD + columns]
    return (centre - average) / jnp.sqrt(spread + 1.0)


def sequence_best(normal_ext, slopes, q_count, m_count):
    sessions = normal_ext.shape[0]
    best_val = None
    for slope_index in range(slopes.shape[0]):
        velocity = slopes[slope_index]
        summed = jnp.zeros((sessions, q_count, m_count), jnp.float32)
        for lag_step in range(SEQ):
            row_at = jnp.asarray(SEQ - 1 - lag_step, jnp.int32)
            col_at = SPAN - lag_step * velocity
            zero_at = jnp.asarray(0, jnp.int32)
            summed = summed + lax.dynamic_slice(
                normal_ext, (zero_at, row_at, col_at), (sessions, q_count, m_count)
            )
        best_val = summed if best_val is None else jnp.maximum(best_val, summed)
    return best_val / math.sqrt(SEQ)


def local(queries, map_descriptors, slopes):
    m_count = map_descriptors.shape[0]
    lead_rows = SEQ - 1
    scores = score_tile(queries, map_descriptors)
    q_count = scores.shape[1]
    widened = padded(scores, (("ma", 2),), RAD)
    normal = contrast(widened, m_count)
    before = passed_along(normal[:, :, m_count - SPAN :], "ma", 1)
    normal_ext = jnp.concatenate([before, normal], axis=2)
    above = passed_along(normal_ext[:, q_count - lead_rows :], "pb", 1)
    normal_ext = jnp.concatenate([above, normal_ext], axis=1)
    return sequence_best(normal_ext, slopes, q_count, m_count)


def solution(mesh):
    return jax.shard_map(
        local,
        mesh=mesh,
        in_specs=(P(None, ("pb", "ma"), None), P("ma", "pb"), P()),
        out_specs=P(None, "pb", "ma"),
        check_vma=False,
    )
```

profile of v0, /device:TPU:1, one launch (start us, length us, event | category | flops | bytes accessed | tf_op | source)
XLA Modules:
  0.0 369.5 jit_solution(10224925232081690869)
XLA Ops:
  6.5 0.0 all-gather.3.cloned.1.call-start
  6.5 0.7 all-gather.3.cloned.1.call-update
  7.3 0.0 all-gather.5.cloned.1.call-start
  7.3 0.7 all-gather.5.cloned.1.call-update
  8.0 42.1 %all-gather.3.cloned.1.call-done = bf16[1,256,2048]{2,1,0:T(8,128)(2,1)} async-done(((bf16[1,32,2048]{2,1,0:T(8,128)(2,1)}), bf16[1,256,2048]{2,1,0:T(8,128)(2,1)}) %all-gather.3.cloned.1.call-update) | async-done | bytes 1048592 | tf_op jit(solution)/shard_map/all_gather | solution.py:32
  50.1 36.9 %all-gather.5.cloned.1.call-done = bf16[1024,2048]{1,0:T(8,128)(2,1)} async-done(((bf16[1024,512]{1,0:T(8,128)(2,1)}), bf16[1024,2048]{1,0:T(8,128)(2,1)}) %all-gather.5.cloned.1.call-update) | async-done | bytes 4194320 | tf_op jit(solution)/shard_map/all_gather | solution.py:36
  87.0 3.8 %fusion.345 = f32[256,1024]{1,0:T(8,128)S(1)} fusion(bf16[1024,2048]{1,0:T(8,128)(2,1)} %all-gather.5.cloned.1.call-done, bf16[1,256,2048]{2,1,0:T(8,128)(2,1)} %all-gather.3.cloned.1.call-done), kind=kOutput, calls=%fused_computation.539 | convolution fusion | flops 1073741824 | bytes 6291456 | tf_op jit(solution)/shard_map/sqd,md->sqm/dot_general | solution.py:33
  90.8 0.1 fusion.348
  90.9 3.1 collective-permute-start
  94.0 0.0 copy-start
  94.0 1.3 collective-permute-start.1
  95.3 1.2 collective-permute-done
  96.6 3.9 %collective-permute-done.1 = f32[1,256,10]{2,1,0:T(8,128)S(1)} collective-permute-done((f32[1,256,10]{2,1,0:T(8,128)S(1)}, f32[1,256,10]{2,1,0:T(8,128)S(1)}, u32[]{:S(2)}, u32[]{:S(2)}) %collective-permute-start.1) | collective-permute-done | bytes 10272 | tf_op jit(solution)/shard_map/ppermute | solution.py:20
  100.4 7.6 %fusion.344 = f32[1,256,1024]{2,1,0:T(8,128)S(1)} fusion(f32[256,1024]{1,0:T(8,128)S(1)} %fusion.345, f32[1,256,1024]{2,1,0:T(8,128)S(1)} %bitcast.342, f32[1,256,10]{2,1,0:T(8,128)S(1)} %collective-permute-done.1, f32[1,256,10]{2,1,0:T(8,128)S(1)} %collective-permute-done), kind=kLoop, calls=%fused_computation.538 | loop fusion | flops 23068672 | bytes 3166208 | tf_op jit(solution)/shard_map/div | solution.py:52
  108.0 0.2 slice.186
  108.2 4.0 %collective-permute-start.2 = (f32[1,256,285]{2,1,0:T(8,128)S(1)}, f32[1,256,285]{2,1,0:T(8,128)S(1)}, u32[]{:S(2)}, u32[]{:S(2)}) collective-permute-start(f32[1,256,285]{2,1,0:T(8,128)S(1)} %slice.186), channel_id=1, source_target_pairs={{0,1},{1,2},{2,3},{3,4},{4,5},{5,6},{6,7},{8,9},{9,10},{10,11},{11... | collective-permute-start | bytes 875528 | tf_op jit(solution)/shard_map/ppermute | solution.py:28
  112.2 0.0 copy-done
  112.2 0.7 fusion.349
  215.6 0.0 collective-permute-done.2
  215.6 0.1 fusion.347
  215.8 3.8 %collective-permute-start.3 = (f32[1,19,1309]{2,1,0:T(8,128)S(1)}, f32[1,19,1309]{2,1,0:T(8,128)S(1)}, u32[]{:S(2)}, u32[]{:S(2)}) collective-permute-start(f32[1,19,1309]{2,1,0:T(8,128)S(1)} %fusion.347), channel_id=1, source_target_pairs={{0,8},{8,16},{16,24},{1,9},{9,17},{17,25},{2,10},{10,18},{18,26},{... | collective-permute-start | bytes 298460 | tf_op jit(solution)/shard_map/ppermute | solution.py:28
  219.5 0.4 pad_maximum_fusion
  219.9 1.6 collective-permute-done.3
  221.5 141.2 %fusion.21 = f32[1,256,1024]{2,1,0:T(8,128)} fusion(s32[]{:T(128)S(6)} %select_n.607, f32[1,19,1309]{2,1,0:T(8,128)S(1)} %collective-permute-done.3, f32[1,256,1024]{2,1,0:T(8,128)S(1)} %fusion.344, s32[]{:T(128)S(6)} %select_n.532, s32[]{:T(128)S(6)} %select_n.533, s32[]{:T(128)S(6)} %select_n.534, s32[]{:T(128)S(6)} %select_n.535, s32[]{:T(128)S(6)} %select_n.536, ...), kind=kLoop, calls=%fused_computation.212 | loop fusion | flops 81788928 | bytes 3537660 | tf_op jit(solution)/shard_map/div | solution.py:69
Async XLA Ops:
  6.5 43.6 %all-gather.3.cloned.1.call-start = ((), (), s32[]{:S(2)}) async-start(), calls=%async_computation | async-start | bytes 1179648 | tf_op jit(solution)/shard_map/all_gather | solution.py:32
  7.3 79.7 %all-gather.5.cloned.1.call-start = ((), (), s32[]{:S(2)}) async-start(), calls=%async_computation.1 | async-start | bytes 5242880 | tf_op jit(solution)/shard_map/all_gather | solution.py:36
  90.9 5.7 %collective-permute-start = (f32[1,256,10]{2,1,0:T(8,128)S(1)}, f32[1,256,10]{2,1,0:T(8,128)S(1)}, u32[]{:S(2)}, u32[]{:S(2)}) collective-permute-start(f32[1,256,10]{2,1,0:T(8,128)S(1)} %get-tuple-element.5), channel_id=1, source_target_pairs={{0,1},{1,2},{2,3},{3,4},{4,5},{5,6},{6,7},{8,9},{9,10},{10,11},{11... | collective-permute-start | bytes 30728 | tf_op jit(solution)/shard_map/ppermute | solution.py:19
  94.0 18.2 %copy-start = (s32[8]{0:T(128)S(1)}, s32[8]{0:T(128)}, u32[]{:S(2)}) copy-start(s32[8]{0:T(128)} %param.5) | copy-start | bytes 100
  94.0 6.4 %collective-permute-start.1 = (f32[1,256,10]{2,1,0:T(8,128)S(1)}, f32[1,256,10]{2,1,0:T(8,128)S(1)}, u32[]{:S(2)}, u32[]{:S(2)}) collective-permute-start(f32[1,256,10]{2,1,0:T(8,128)S(1)} %get-tuple-element.6), channel_id=1, source_target_pairs={{1,0},{2,1},{3,2},{4,3},{5,4},{6,5},{7,6},{9,8},{10,9},{11,10},{12... | collective-permute-start | bytes 30728 | tf_op jit(solution)/shard_map/ppermute | solution.py:20
  108.2 107.5 %collective-permute-start.2 = (f32[1,256,285]{2,1,0:T(8,128)S(1)}, f32[1,256,285]{2,1,0:T(8,128)S(1)}, u32[]{:S(2)}, u32[]{:S(2)}) collective-permute-start(f32[1,256,285]{2,1,0:T(8,128)S(1)} %slice.186), channel_id=1, source_target_pairs={{0,1},{1,2},{2,3},{3,4},{4,5},{5,6},{6,7},{8,9},{9,10},{10,11},{11... | collective-permute-start | bytes 875528 | tf_op jit(solution)/shard_map/ppermute | solution.py:28
  215.8 5.7 %collective-permute-start.3 = (f32[1,19,1309]{2,1,0:T(8,128)S(1)}, f32[1,19,1309]{2,1,0:T(8,128)S(1)}, u32[]{:S(2)}, u32[]{:S(2)}) collective-permute-start(f32[1,19,1309]{2,1,0:T(8,128)S(1)} %fusion.347), channel_id=1, source_target_pairs={{0,8},{8,16},{16,24},{1,9},{9,17},{17,25},{2,10},{10,18},{18,26},{... | collective-permute-start | bytes 298460 | tf_op jit(solution)/shard_map/ppermute | solution.py:28
Sparse Core Ops, SparseCore 0:
  9.5 40.6 all-gather.2
  51.7 35.2 all-gather.4
where the time goes:
time: 371 us; the launch traced here: 370 us
  other arithmetic  149 us (40%)
  between operations  116 us (31%)
  waiting for transfers between devices  87.1 us (23%)
  starting transfers between devices  12.2 us (3%)
  matrix products  3.79 us (1%)
    div x1, other arithmetic, sequence_best(): return best_val / math.sqrt(SEQ)  141 us
    all_gather x1, waiting for transfers between devices, score_tile(): query_full = lax.all_gather(queries, 'ma', axis=1, tiled=True)  42.1 us
    all_gather x1, waiting for transfers between devices, score_tile(): lax.all_gather(map_descriptors, 'pb', axis=1, tiled=True)  36.9 us
    ppermute x2, starting transfers between devices, passed_along(): return lax.ppermute(value, axis, pairs)  7.78 us
    div x1, other arithmetic, contrast(): return (centre - average) / jnp.sqrt(spread + 1.0)  7.57 us
  transfers between devices with their start and end apart: 6, of which 5 were waited for; matrix products, arithmetic and copies ran while one was open for 0% of the time, Pallas kernels for 0%

commit v1 on v0

--- a/solution.py
+++ b/solution.py
@@ -29,7 +29,36 @@
 
 
 def score_tile(queries, map_descriptors):
-    query_full = lax.all_gather(queries, "ma", axis=1, tiled=True)
+    state_now, earlier, piece_next = (lax.axis_size("ma"), lax.axis_index("ma"), queries.shape[1])
+    seen = []
+    for dev_i, j0 in enumerate(queries.shape):
+        seen.append(j0 * state_now if dev_i == 1 else j0)
+    query_full = lax.dynamic_update_slice_in_dim(
+        jnp.zeros(seen, queries.dtype), queries, earlier * piece_next, axis=1
+    )
+    response = low = queries
+    jj = 1
+    while jj < state_now // 2 + 1:
+        xs_all = []
+        dev_i = 0
+        while dev_i < state_now:
+            xs_all.append((dev_i, (dev_i + 1) % state_now))
+            dev_i += 1
+        response = lax.ppermute(response, "ma", xs_all)
+        query_full = lax.dynamic_update_slice_in_dim(
+            query_full, response, (earlier - jj) % state_now * piece_next, axis=1
+        )
+        if 2 * jj < state_now:
+            found = []
+            dev_i = 0
+            while dev_i < state_now:
+                found.append((dev_i, (dev_i - 1) % state_now))
+                dev_i += 1
+            low = lax.ppermute(low, "ma", found)
+            query_full = lax.dynamic_update_slice_in_dim(
+                query_full, low, (earlier + jj) % state_now * piece_next, axis=1
+            )
+        jj += 1
     return jnp.einsum(
         "sqd,md->sqm",
         query_full,

time: 371 us -> 329 us (0.89)
  waiting for transfers between devices: 87.1 us -> 31.6 us
  starting transfers between devices: 12.2 us -> 26.1 us
    all_gather x1 -> x0, waiting for transfers between devices: 42.1 us -> none  [score_tile(): query_full = lax.all_gather(queries, 'ma', axis=1, tiled=True)]
    all_gather x1, waiting for transfers between devices: 36.9 us -> 10.4 us  [score_tile(): lax.all_gather(map_descriptors, 'pb', axis=1, tiled=True)]
    ppermute x0 -> x7, starting transfers between devices: none -> 13.9 us  [the longest x3 11.9 us: score_tile(): low = lax.ppermute(low, 'ma', found)]
    ppermute x0 -> x7, waiting for transfers between devices: none -> 13.8 us  [the longest x4 13.8 us: score_tile(): response = lax.ppermute(response, 'ma', xs_all)]
  transfers between devices with their start and end apart: 6 -> 12, of which waited for: 5 -> 8; matrix products, arithmetic and copies ran while one was open for 0% -> 0% of each run, Pallas kernels for 0% -> 0%
where the time goes in v1:
time: 329 us; the launch traced here: 327 us
  other arithmetic  149 us (45%)
  between operations  116 us (35%)
  waiting for transfers between devices  31.6 us (10%)
  starting transfers between devices  26.1 us (8%)
  matrix products  3.46 us (1%)
    div x1, other arithmetic, sequence_best(): return best_val / math.sqrt(SEQ)  141 us
    ppermute x4, waiting for transfers between devices, score_tile(): response = lax.ppermute(response, 'ma', xs_all)  13.8 us
    ppermute x3, starting transfers between devices, score_tile(): low = lax.ppermute(low, 'ma', found)  11.9 us
    all_gather x1, waiting for transfers between devices, score_tile(): lax.all_gather(map_descriptors, 'pb', axis=1, tiled=True)  10.4 us
    ppermute x2, starting transfers between devices, passed_along(): return lax.ppermute(value, axis, pairs)  7.78 us
    div x1, other arithmetic, contrast(): return (centre - average) / jnp.sqrt(spread + 1.0)  7.57 us
  transfers between devices with their start and end apart: 12, of which 8 were waited for; matrix products, arithmetic and copies ran while one was open for 0% of the time, Pallas kernels for 0%

profile of v1, /device:TPU:1, one launch (start us, length us, event | category | flops | bytes accessed | tf_op | source)
XLA Modules:
  0.0 327.2 jit_solution(874782434138649852)
XLA Ops:
  6.5 0.7 all-gather.2.cloned.1.call-update
  7.3 2.1 collective-permute-start
  9.3 3.1 collective-permute-start.1
  12.4 0.1 broadcast.17
  12.7 3.1 collective-permute-done
  15.8 4.2 %collective-permute-start.3 = (bf16[1,32,2048]{2,1,0:T(8,128)(2,1)S(1)}, bf16[1,32,2048]{2,1,0:T(8,128)(2,1)S(1)}, u32[]{:S(2)}, u32[]{:S(2)}) collective-permute-start(bf16[1,32,2048]{2,1,0:T(8,128)(2,1)S(1)} %collective-permute-done.1), channel_id=1, source_target_pairs={{0,7},{1,0},{2,1},{3,2},{4,3},{5,4},{6,5},{7,6},{8,15},{9,8},{10,9... | collective-permute-start | bytes 393224 | tf_op jit(solution)/shard_map/ppermute | solution.py:57
  20.0 2.4 collective-permute-done.2
  22.4 4.6 %collective-permute-start.5 = (bf16[1,32,2048]{2,1,0:T(8,128)(2,1)S(1)}, bf16[1,32,2048]{2,1,0:T(8,128)(2,1)S(1)}, u32[]{:S(2)}, u32[]{:S(2)}) collective-permute-start(bf16[1,32,2048]{2,1,0:T(8,128)(2,1)S(1)} %collective-permute-done.3), channel_id=1, source_target_pairs={{0,7},{1,0},{2,1},{3,2},{4,3},{5,4},{6,5},{7,6},{8,15},{9,8},{10,9... | collective-permute-start | bytes 393224 | tf_op jit(solution)/shard_map/ppermute | solution.py:57
  27.0 1.9 collective-permute-done.4
  29.0 6.5 %collective-permute-done.6 = bf16[1,32,2048]{2,1,0:T(8,128)(2,1)S(1)} collective-permute-done((bf16[1,32,2048]{2,1,0:T(8,128)(2,1)S(1)}, bf16[1,32,2048]{2,1,0:T(8,128)(2,1)S(1)}, u32[]{:S(2)}, u32[]{:S(2)}) %collective-permute-start.6) | collective-permute-done | bytes 131104 | tf_op jit(solution)/shard_map/ppermute | solution.py:47
  35.4 10.4 %all-gather.2.cloned.1.call-done = bf16[1024,2048]{1,0:T(8,128)(2,1)} async-done(((bf16[1024,512]{1,0:T(8,128)(2,1)}), bf16[1024,2048]{1,0:T(8,128)(2,1)}) %all-gather.2.cloned.1.call-update) | async-done | bytes 4194320 | tf_op jit(solution)/shard_map/all_gather | solution.py:65
  45.9 3.5 %fusion.348 = f32[256,1024]{1,0:T(8,128)S(1)} fusion(bf16[256,2048]{1,0:T(8,128)(2,1)S(1)} %bitcast_dynamic-update-slice_fusion, bf16[1024,2048]{1,0:T(8,128)(2,1)} %all-gather.2.cloned.1.call-done), kind=kOutput, calls=%fused_computation.606 | convolution fusion | flops 1073741824 | bytes 6291456 | tf_op jit(solution)/shard_map/sqd,md->sqm/dot_general | solution.py:62
  49.4 3.1 collective-permute-start.7
  52.5 1.3 collective-permute-start.8
  53.8 1.2 collective-permute-done.7
  55.1 3.9 %collective-permute-done.8 = f32[1,256,10]{2,1,0:T(8,128)S(1)} collective-permute-done((f32[1,256,10]{2,1,0:T(8,128)S(1)}, f32[1,256,10]{2,1,0:T(8,128)S(1)}, u32[]{:S(2)}, u32[]{:S(2)}) %collective-permute-start.8) | collective-permute-done | bytes 10272 | tf_op jit(solution)/shard_map/ppermute | solution.py:20
  58.9 7.6 %fusion.344 = f32[1,256,1024]{2,1,0:T(8,128)S(1)} fusion(f32[256,1024]{1,0:T(8,128)S(1)} %fusion.348, f32[1,256,1024]{2,1,0:T(8,128)S(1)} %bitcast.356, f32[1,256,10]{2,1,0:T(8,128)S(1)} %collective-permute-done.8, f32[1,256,10]{2,1,0:T(8,128)S(1)} %collective-permute-done.7), kind=kLoop, calls=%fused_computation.538 | loop fusion | flops 23068672 | bytes 3166208 | tf_op jit(solution)/shard_map/div | solution.py:81
  66.5 0.2 slice.186
  66.7 4.0 %collective-permute-start.9 = (f32[1,256,285]{2,1,0:T(8,128)S(1)}, f32[1,256,285]{2,1,0:T(8,128)S(1)}, u32[]{:S(2)}, u32[]{:S(2)}) collective-permute-start(f32[1,256,285]{2,1,0:T(8,128)S(1)} %slice.186), channel_id=1, source_target_pairs={{0,1},{1,2},{2,3},{3,4},{4,5},{5,6},{6,7},{8,9},{9,10},{10,11},{11... | collective-permute-start | bytes 875528 | tf_op jit(solution)/shard_map/ppermute | solution.py:28
  70.7 0.7 fusion.347
  173.4 3.8 %collective-permute-start.10 = (f32[1,19,1309]{2,1,0:T(8,128)S(1)}, f32[1,19,1309]{2,1,0:T(8,128)S(1)}, u32[]{:S(2)}, u32[]{:S(2)}) collective-permute-start(f32[1,19,1309]{2,1,0:T(8,128)S(1)} %fusion.345), channel_id=1, source_target_pairs={{0,8},{8,16},{16,24},{1,9},{9,17},{17,25},{2,10},{10,18},{18,26},{... | collective-permute-start | bytes 298460 | tf_op jit(solution)/shard_map/ppermute | solution.py:28
  177.2 0.4 pad_maximum_fusion
  177.6 1.6 collective-permute-done.10
  179.2 141.2 %fusion.21 = f32[1,256,1024]{2,1,0:T(8,128)} fusion(s32[]{:T(128)S(6)} %select_n.677, f32[1,19,1309]{2,1,0:T(8,128)S(1)} %collective-permute-done.10, f32[1,256,1024]{2,1,0:T(8,128)S(1)} %fusion.344, s32[]{:T(128)S(6)} %select_n.602, s32[]{:T(128)S(6)} %select_n.603, s32[]{:T(128)S(6)} %select_n.604, s32[]{:T(128)S(6)} %select_n.605, s32[]{:T(128)S(6)} %select_n.606, ...), kind=kLoop, calls=%fused_computation.212 | loop fusion | flops 81788928 | bytes 3537660 | tf_op jit(solution)/shard_map/div | solution.py:98
  (22 shorter events, 0.3 us)
Async XLA Ops:
  6.5 6.0 %copy-start = (bf16[1,32,2048]{2,1,0:T(8,128)(2,1)S(1)}, bf16[1,32,2048]{2,1,0:T(8,128)(2,1)}, u32[]{:S(2)}) copy-start(bf16[1,32,2048]{2,1,0:T(8,128)(2,1)} %param.3) | copy-start | bytes 393220
  6.5 39.3 %all-gather.2.cloned.1.call-start = ((), (), s32[]{:S(2)}) async-start(), calls=%async_computation | async-start | bytes 5242880 | tf_op jit(solution)/shard_map/all_gather | solution.py:65
  7.3 8.5 %collective-permute-start = (bf16[1,32,2048]{2,1,0:T(8,128)(2,1)}, bf16[1,32,2048]{2,1,0:T(8,128)(2,1)S(1)}, u32[]{:S(2)}, u32[]{:S(2)}) collective-permute-start(bf16[1,32,2048]{2,1,0:T(8,128)(2,1)} %param.3), channel_id=1, source_target_pairs={{0,1},{1,2},{2,3},{3,4},{4,5},{5,6},{6,7},{7,0},{8,9},{9,10},{10,1... | collective-permute-start | bytes 393224 | tf_op jit(solution)/shard_map/ppermute | solution.py:47
  9.3 6.5 %collective-permute-start.1 = (bf16[1,32,2048]{2,1,0:T(8,128)(2,1)}, bf16[1,32,2048]{2,1,0:T(8,128)(2,1)S(1)}, u32[]{:S(2)}, u32[]{:S(2)}) collective-permute-start(bf16[1,32,2048]{2,1,0:T(8,128)(2,1)} %param.3), channel_id=1, source_target_pairs={{0,7},{1,0},{2,1},{3,2},{4,3},{5,4},{6,5},{7,6},{8,15},{9,8},{10,9... | collective-permute-start | bytes 393224 | tf_op jit(solution)/shard_map/ppermute | solution.py:57
  15.8 6.6 %collective-permute-start.2 = (bf16[1,32,2048]{2,1,0:T(8,128)(2,1)S(1)}, bf16[1,32,2048]{2,1,0:T(8,128)(2,1)S(1)}, u32[]{:S(2)}, u32[]{:S(2)}) collective-permute-start(bf16[1,32,2048]{2,1,0:T(8,128)(2,1)S(1)} %collective-permute-done), channel_id=1, source_target_pairs={{0,1},{1,2},{2,3},{3,4},{4,5},{5,6},{6,7},{7,0},{8,9},{9,10},{10,1... | collective-permute-start | bytes 393224 | tf_op jit(solution)/shard_map/ppermute | solution.py:47
  15.8 6.6 %collective-permute-start.3 = (bf16[1,32,2048]{2,1,0:T(8,128)(2,1)S(1)}, bf16[1,32,2048]{2,1,0:T(8,128)(2,1)S(1)}, u32[]{:S(2)}, u32[]{:S(2)}) collective-permute-start(bf16[1,32,2048]{2,1,0:T(8,128)(2,1)S(1)} %collective-permute-done.1), channel_id=1, source_target_pairs={{0,7},{1,0},{2,1},{3,2},{4,3},{5,4},{6,5},{7,6},{8,15},{9,8},{10,9... | collective-permute-start | bytes 393224 | tf_op jit(solution)/shard_map/ppermute | solution.py:57
  22.4 6.5 %collective-permute-start.4 = (bf16[1,32,2048]{2,1,0:T(8,128)(2,1)S(1)}, bf16[1,32,2048]{2,1,0:T(8,128)(2,1)S(1)}, u32[]{:S(2)}, u32[]{:S(2)}) collective-permute-start(bf16[1,32,2048]{2,1,0:T(8,128)(2,1)S(1)} %collective-permute-done.2), channel_id=1, source_target_pairs={{0,1},{1,2},{2,3},{3,4},{4,5},{5,6},{6,7},{7,0},{8,9},{9,10},{10,1... | collective-permute-start | bytes 393224 | tf_op jit(solution)/shard_map/ppermute | solution.py:47
  22.4 6.5 %collective-permute-start.5 = (bf16[1,32,2048]{2,1,0:T(8,128)(2,1)S(1)}, bf16[1,32,2048]{2,1,0:T(8,128)(2,1)S(1)}, u32[]{:S(2)}, u32[]{:S(2)}) collective-permute-start(bf16[1,32,2048]{2,1,0:T(8,128)(2,1)S(1)} %collective-permute-done.3), channel_id=1, source_target_pairs={{0,7},{1,0},{2,1},{3,2},{4,3},{5,4},{6,5},{7,6},{8,15},{9,8},{10,9... | collective-permute-start | bytes 393224 | tf_op jit(solution)/shard_map/ppermute | solution.py:57
  28.9 6.5 %collective-permute-start.6 = (bf16[1,32,2048]{2,1,0:T(8,128)(2,1)S(1)}, bf16[1,32,2048]{2,1,0:T(8,128)(2,1)S(1)}, u32[]{:S(2)}, u32[]{:S(2)}) collective-permute-start(bf16[1,32,2048]{2,1,0:T(8,128)(2,1)S(1)} %collective-permute-done.4), channel_id=1, source_target_pairs={{0,1},{1,2},{2,3},{3,4},{4,5},{5,6},{6,7},{7,0},{8,9},{9,10},{10,1... | collective-permute-start | bytes 393224 | tf_op jit(solution)/shard_map/ppermute | solution.py:47
  49.4 5.7 %collective-permute-start.7 = (f32[1,256,10]{2,1,0:T(8,128)S(1)}, f32[1,256,10]{2,1,0:T(8,128)S(1)}, u32[]{:S(2)}, u32[]{:S(2)}) collective-permute-start(f32[1,256,10]{2,1,0:T(8,128)S(1)} %get-tuple-element.5), channel_id=1, source_target_pairs={{0,1},{1,2},{2,3},{3,4},{4,5},{5,6},{6,7},{8,9},{9,10},{10,11},{11... | collective-permute-start | bytes 30728 | tf_op jit(solution)/shard_map/ppermute | solution.py:19
  52.5 18.2 %copy-start.1 = (s32[8]{0:T(128)S(1)}, s32[8]{0:T(128)}, u32[]{:S(2)}) copy-start(s32[8]{0:T(128)} %param.5) | copy-start | bytes 100
  52.5 6.4 %collective-permute-start.8 = (f32[1,256,10]{2,1,0:T(8,128)S(1)}, f32[1,256,10]{2,1,0:T(8,128)S(1)}, u32[]{:S(2)}, u32[]{:S(2)}) collective-permute-start(f32[1,256,10]{2,1,0:T(8,128)S(1)} %get-tuple-element.6), channel_id=1, source_target_pairs={{1,0},{2,1},{3,2},{4,3},{5,4},{6,5},{7,6},{9,8},{10,9},{11,10},{12... | collective-permute-start | bytes 30728 | tf_op jit(solution)/shard_map/ppermute | solution.py:20
  66.7 106.6 %collective-permute-start.9 = (f32[1,256,285]{2,1,0:T(8,128)S(1)}, f32[1,256,285]{2,1,0:T(8,128)S(1)}, u32[]{:S(2)}, u32[]{:S(2)}) collective-permute-start(f32[1,256,285]{2,1,0:T(8,128)S(1)} %slice.186), channel_id=1, source_target_pairs={{0,1},{1,2},{2,3},{3,4},{4,5},{5,6},{6,7},{8,9},{9,10},{10,11},{11... | collective-permute-start | bytes 875528 | tf_op jit(solution)/shard_map/ppermute | solution.py:28
  173.4 5.7 %collective-permute-start.10 = (f32[1,19,1309]{2,1,0:T(8,128)S(1)}, f32[1,19,1309]{2,1,0:T(8,128)S(1)}, u32[]{:S(2)}, u32[]{:S(2)}) collective-permute-start(f32[1,19,1309]{2,1,0:T(8,128)S(1)} %fusion.345), channel_id=1, source_target_pairs={{0,8},{8,16},{16,24},{1,9},{9,17},{17,25},{2,10},{10,18},{18,26},{... | collective-permute-start | bytes 298460 | tf_op jit(solution)/shard_map/ppermute | solution.py:28
Sparse Core Ops, SparseCore 0:
  8.9 36.9 all-gather.1
